TPU v7x, 32 devices: a whole 2x2x4 slice. The times are simulated.
32 devices in a mesh: dp: 4 (over y, x), ctx: 8 (over z, core).
Axes of the slice: x: 2, y: 2, z: 4, core: 2. Of those that a mesh axis runs over, the one named last changes fastest.
Arguments:
- inputs: bfloat16 [4, 1024, 4096], P('dp', 'ctx'), may hold values from -8 to 8
- queries: bfloat16 [4, 1024, 8192], P('dp', 'ctx'), may hold values from -256 to 256
- grad_output: bfloat16 [4, 1024, 8192], P('dp', 'ctx'), may hold values from -6 to 6
- kv_weight: bfloat16 [4096, 1024], P(('dp', 'ctx')), may hold values from -1 to 1
Outputs:
- attn_out: bfloat16 [4, 1024, 8192], P('dp', 'ctx')
- grad_query: bfloat16 [4, 1024, 8192], P('dp', 'ctx')
- grad_inputs: bfloat16 [4, 1024, 4096], P('dp', 'ctx')
- grad_weight: float32 [4096, 1024], P(('dp', 'ctx'))
All inputs are finite; a program needn't handle non-finite values.
Results may differ from a plain program's by a relative error of at most 0.035.
Values may be sent and summed in bfloat16 or wider, within the bound.
No kernel may reach another device: no remote copies, remote signals or barrier semaphores. Data moves between devices by JAX's collectives and lax.ppermute only.
A program may use at most 128 MiB of HBM per device.

v0:
```python
import jax
import jax.numpy as jnp
from jax import lax
from jax.sharding import PartitionSpec as P

DH = 128
ROPE_BASE = 500000.0


def shifted(block, axis, distance):
    devices = range(lax.axis_size(axis))
    route = [(i - distance, i) for i in devices if i - distance in devices]
    return lax.ppermute(block, axis, route)


def shifted_2(value, axis, steps):
    count = lax.axis_size(axis)
    pairs = [(source, (source + steps) % count) for source in range(count)]
    return lax.ppermute(value, axis, pairs)


def rope_tables(positions, head_dim):
    half_dim = head_dim // 2
    frequency = ROPE_BASE ** (-2.0 * jnp.arange(half_dim, dtype=jnp.float32) / head_dim)
    angles = positions.astype(jnp.float32)[:, None] * frequency[None, :]
    return (jnp.cos(angles)[:, None, :], jnp.sin(angles)[:, None, :])


def rotary(values, positions):
    half_dim = values.shape[-1] // 2
    cosine, sine_table = rope_tables(positions, values.shape[-1])
    first_half = values[..., :half_dim]
    second = values[..., half_dim:]
    return jnp.concatenate(
        [first_half * cosine - second * sine_table, second * cosine + first_half * sine_table],
        axis=-1,
    )


def rotary_back(gradient, positions):
    half_dim = gradient.shape[-1] // 2
    cosine, sine_table = rope_tables(positions, gradient.shape[-1])
    first_half = gradient[..., :half_dim]
    second = gradient[..., half_dim:]
    return jnp.concatenate(
        [first_half * cosine + second * sine_table, second * cosine - first_half * sine_table],
        axis=-1,
    )


def on_device(inputs, queries, grad_output, kv_weight):
    token_count = inputs.shape[1]
    model_width = inputs.shape[2]
    kv_width = kv_weight.shape[1]
    kv_half = kv_width // 2
    head_dim = DH
    kv_heads = kv_half // head_dim
    q_heads = queries.shape[2] // head_dim
    group_size = q_heads // kv_heads
    row_count = group_size * token_count
    ctx_size = lax.axis_size("ctx")
    data_size = lax.axis_size("dp")
    ctx_index = lax.axis_index("ctx")
    score_scale = head_dim ** (-0.5)
    shard_rows = model_width // (data_size * ctx_size)
    tokens = inputs[0]
    weight_all = lax.all_gather(kv_weight, ("dp", "ctx"), axis=0, tiled=True)
    projected = jnp.dot(tokens, weight_all, preferred_element_type=jnp.float32)
    positions = ctx_index * token_count + jnp.arange(token_count, dtype=jnp.int32)
    key_rows = rotary(
        projected[:, :kv_half].reshape(token_count, kv_heads, head_dim), positions
    ).astype(jnp.bfloat16)
    value_rows = projected[:, kv_half:].astype(jnp.bfloat16)
    own_block = jnp.concatenate([key_rows.reshape(token_count, kv_half), value_rows], axis=1)

    def head_rows(matrix):
        return (
            matrix.reshape(token_count, kv_heads, group_size, head_dim)
            .transpose(1, 2, 0, 3)
            .reshape(kv_heads, row_count, head_dim)
        )

    def token_rows(rows_by_head):
        return (
            rows_by_head.reshape(kv_heads, group_size, token_count, head_dim)
            .transpose(2, 0, 1, 3)
            .reshape(token_count, q_heads * head_dim)
        )

    query_rows = head_rows(queries[0])
    grad_rows = head_rows(grad_output[0])
    query_pos = jnp.arange(row_count, dtype=jnp.int32) % token_count
    key_pos = jnp.arange(token_count, dtype=jnp.int32)

    def split_block(kv_block):
        key_part = kv_block[:, :kv_half].reshape(token_count, kv_heads, head_dim)
        value_part = kv_block[:, kv_half:].reshape(token_count, kv_heads, head_dim)
        return (key_part, value_part)

    def block_scores(key_part, block_id):
        scores = (
            jnp.einsum("hrd,khd->hrk", query_rows, key_part, preferred_element_type=jnp.float32)
            * score_scale
        )
        allowed = (block_id < ctx_index) | (query_pos[:, None] >= key_pos[None, :])
        return (scores, allowed)

    def forward_update(state_now, kv_block, block_id):
        row_top, row_total, row_accum = state_now
        key_part, value_part = split_block(kv_block)
        scores, allowed = block_scores(key_part, block_id)
        scores = jnp.where(allowed[None], scores, -jnp.inf)
        new_top = jnp.maximum(row_top, jnp.max(scores, axis=-1, keepdims=True))
        weights = jnp.exp(scores - new_top)
        factor = jnp.exp(row_top - new_top)
        row_total = row_total * factor + jnp.sum(weights, axis=-1, keepdims=True)
        row_accum = row_accum * factor + jnp.einsum(
            "hrk,khd->hrd",
            weights.astype(jnp.bfloat16),
            value_part,
            preferred_element_type=jnp.float32,
        )
        return (new_top, row_total, row_accum)

    start_state = (
        jnp.full((kv_heads, row_count, 1), -jnp.inf, jnp.float32),
        jnp.zeros((kv_heads, row_count, 1), jnp.float32),
        jnp.zeros((kv_heads, row_count, head_dim), jnp.float32),
    )
    state_now = forward_update(start_state, own_block, ctx_index)
    kv_store = jnp.zeros((ctx_size, token_count, kv_width), jnp.bfloat16)
    kv_store = lax.dynamic_update_slice_in_dim(kv_store, own_block[None], ctx_index, 0)

    def forward_step(offset, loop_state):
        kv_block, stored_now, state_here = loop_state
        kv_block = shifted(kv_block, "ctx", 1)
        source = ctx_index - offset

        def take_block(operands):
            stored, current = operands
            stored = lax.dynamic_update_slice_in_dim(stored, kv_block[None], source, 0)
            return (stored, forward_update(current, kv_block, source))

        def keep_state(operands):
            return operands

        stored_now, state_here = lax.cond(
            offset <= ctx_index, take_block, keep_state, (stored_now, state_here)
        )
        return (kv_block, stored_now, state_here)

    last_block, kv_store, state_now = lax.fori_loop(
        1, ctx_size, forward_step, (own_block, kv_store, state_now)
    )
    row_top, row_total, row_accum = state_now
    attn_rows = (row_accum / row_total).astype(jnp.bfloat16)
    log_total = row_top + jnp.log(row_total)
    row_delta = jnp.sum(
        grad_rows.astype(jnp.float32) * attn_rows.astype(jnp.float32), axis=-1, keepdims=True
    )
    attn_out = token_rows(attn_rows)[None]

    def backward_terms(kv_block, block_id):
        key_part, value_part = split_block(kv_block)
        scores, allowed = block_scores(key_part, block_id)
        probs_now = jnp.where(allowed[None], jnp.exp(scores - log_total), 0.0)
        dprobs = jnp.einsum(
            "hrd,khd->hrk", grad_rows, value_part, preferred_element_type=jnp.float32
        )
        dscores = (probs_now * (dprobs - row_delta)).astype(jnp.bfloat16)
        grad_keys = (
            jnp.einsum("hrk,hrd->khd", dscores, query_rows, preferred_element_type=jnp.float32)
            * score_scale
        )
        grad_values = jnp.einsum(
            "hrk,hrd->khd",
            probs_now.astype(jnp.bfloat16),
            grad_rows,
            preferred_element_type=jnp.float32,
        )
        query_part = jnp.einsum(
            "hrk,khd->hrd", dscores, key_part, preferred_element_type=jnp.float32
        )
        block_grads = jnp.concatenate(
            [grad_keys.reshape(token_count, kv_half), grad_values.reshape(token_count, kv_half)],
            axis=1,
        )
        return (block_grads, query_part)

    def add_block(operands, block_id):
        grad_block, grad_query_sum = operands
        kv_block = lax.dynamic_slice_in_dim(kv_store, block_id, 1, 0)[0]
        block_grads, query_part = backward_terms(kv_block, block_id)
        return (grad_block + block_grads, grad_query_sum + query_part)

    def skip_block(operand_pair):
        return operand_pair

    zero_grads = jnp.zeros((token_count, kv_width), jnp.float32)
    zero_query = jnp.zeros((kv_heads, row_count, head_dim), jnp.float32)

    def backward_step(offset, operands):
        source = ctx_index - offset

        def include(operand_pair):
            return add_block(operand_pair, source)

        grad_block, grad_query_sum = lax.cond(offset <= ctx_index, include, skip_block, operands)
        grad_block = shifted_2(grad_block.astype(jnp.bfloat16), "ctx", 1).astype(grad_block.dtype)
        return (grad_block, grad_query_sum)

    grad_block, grad_query_sum = lax.fori_loop(0, ctx_size, backward_step, (zero_grads, zero_query))
    grad_query = token_rows(grad_query_sum * score_scale).astype(jnp.bfloat16)[None]
    grad_key_rows = rotary_back(
        grad_block[:, :kv_half].reshape(token_count, kv_heads, head_dim), positions
    ).reshape(token_count, kv_half)
    grad_projected = jnp.concatenate([grad_key_rows, grad_block[:, kv_half:]], axis=1).astype(
        jnp.bfloat16
    )
    grad_inputs = lax.dot_general(
        grad_projected, weight_all, (((1,), (1,)), ((), ())), preferred_element_type=jnp.float32
    ).astype(jnp.bfloat16)[None]
    reordered = (
        tokens.reshape(token_count, data_size, ctx_size, shard_rows)
        .transpose(0, 2, 1, 3)
        .reshape(token_count, model_width)
    )
    partial_sum = lax.psum_scatter(
        lax.dot_general(
            reordered, grad_projected, (((0,), (0,)), ((), ())), preferred_element_type=jnp.float32
        ).astype(jnp.bfloat16),
        "ctx",
        scatter_dimension=0,
        tiled=True,
    )
    grad_weight = lax.psum_scatter(partial_sum, "dp", scatter_dimension=0, tiled=True).astype(
        jnp.float32
    )
    return (attn_out, grad_query, grad_inputs, grad_weight)


def solution(mesh):
    in_specs = (
        P("dp", "ctx", None),
        P("dp", "ctx", None),
        P("dp", "ctx", None),
        P(("dp", "ctx"), None),
    )
    out_specs = (
        P("dp", "ctx", None),
        P("dp", "ctx", None),
        P("dp", "ctx", None),
        P(("dp", "ctx"), None),
    )
    return jax.shard_map(
        on_device, mesh=mesh, in_specs=in_specs, out_specs=out_specs, check_vma=False
    )
```

profile of v0, /device:TPU:0, one launch (start us, length us, event | category | flops | bytes accessed | tf_op | source)
XLA Modules:
  0.0 496.9 jit_solution(8035987753920673615)
XLA Ops:
  8.0 3.5 copy.141
  11.5 4.3 copy.110
  15.8 2.3 reshape.240
  18.1 2.2 copy.139
  20.2 3.8 copy.102
  24.1 2.8 reshape.237
  26.9 2.5 copy.107
  29.4 2.3 copy.115
  31.6 2.3 copy.116
  35.2 55.6 %all-gather.2.cloned.1.call-done = bf16[4096,1024]{1,0:T(8,128)(2,1)} async-done(((bf16[128,1024]{1,0:T(8,128)(2,1)}), bf16[4096,1024]{1,0:T(8,128)(2,1)}) %all-gather.2.cloned.1.call-update) | async-done | bytes 8388624 | tf_op jit(solution)/shard_map/all_gather | solution.py:67
  90.8 5.0 fusion.27
  97.1 1.0 reshape.236
  98.6 1.8 fusion.36
  100.4 1.8 copy.106
  102.1 1.8 copy.101
  103.9 2.1 fusion.41
  106.7 3.3 convolution_add_fusion.1
  110.4 1.3 copy-done.5
  111.7 71.5 %while.38 = (s32[]{:T(128)}, bf16[128,1024]{0,1:T(8,128)(2,1)S(1)}, bf16[8,128,1024]{1,2,0:T(8,128)(2,1)}, f32[4,2048,1]{1,0,2:T(4,128)S(1)}, f32[4,2048,1]{1,0,...) while((s32[]{:T(128)}, bf16[128,1024]{0,1:T(8,128)(2,1)S(1)}, ...), condition=%wide.region_7.8_spmd.clone, body=%wide.region_2.7_spmd.clone.sunk | while | flops 551063552 | bytes 61154760 | solution.py:152
  111.7 2.2 collective-permute-start
  113.9 1.1 collective-permute-done
  115.0 15.1 %collective-permute-start = (bf16[128,1024]{0,1:T(8,128)(2,1)S(1)}, bf16[128,1024]{0,1:T(8,128)(2,1)S(1)}, u32[]{:S(2)}, u32[]{:S(2)}) collective-permute-start(bf16[128,1024]{0,1:T(8,128)(2,1)S(1)} %get-tuple-element.850), channel_id=1, source_target_pairs={{0,1},{1,2},{2,3},{3,4},{4,5},{5,6},{6,7},{8,9},{9,10},{10,11},{11... | collective-permute-start | bytes 786440 | tf_op jit(solution)/shard_map/while/body/eval_jaxpr/ppermute | solution.py:13
  130.2 1.1 collective-permute-done
  131.3 6.6 %collective-permute-start = (bf16[128,1024]{0,1:T(8,128)(2,1)S(1)}, bf16[128,1024]{0,1:T(8,128)(2,1)S(1)}, u32[]{:S(2)}, u32[]{:S(2)}) collective-permute-start(bf16[128,1024]{0,1:T(8,128)(2,1)S(1)} %get-tuple-element.850), channel_id=1, source_target_pairs={{0,1},{1,2},{2,3},{3,4},{4,5},{5,6},{6,7},{8,9},{9,10},{10,11},{11... | collective-permute-start | bytes 786440 | tf_op jit(solution)/shard_map/while/body/eval_jaxpr/ppermute | solution.py:13
  137.9 1.1 collective-permute-done
  139.0 16.2 %collective-permute-start = (bf16[128,1024]{0,1:T(8,128)(2,1)S(1)}, bf16[128,1024]{0,1:T(8,128)(2,1)S(1)}, u32[]{:S(2)}, u32[]{:S(2)}) collective-permute-start(bf16[128,1024]{0,1:T(8,128)(2,1)S(1)} %get-tuple-element.850), channel_id=1, source_target_pairs={{0,1},{1,2},{2,3},{3,4},{4,5},{5,6},{6,7},{8,9},{9,10},{10,11},{11... | collective-permute-start | bytes 786440 | tf_op jit(solution)/shard_map/while/body/eval_jaxpr/ppermute | solution.py:13
  155.3 1.1 collective-permute-done
  156.4 6.6 %collective-permute-start = (bf16[128,1024]{0,1:T(8,128)(2,1)S(1)}, bf16[128,1024]{0,1:T(8,128)(2,1)S(1)}, u32[]{:S(2)}, u32[]{:S(2)}) collective-permute-start(bf16[128,1024]{0,1:T(8,128)(2,1)S(1)} %get-tuple-element.850), channel_id=1, source_target_pairs={{0,1},{1,2},{2,3},{3,4},{4,5},{5,6},{6,7},{8,9},{9,10},{10,11},{11... | collective-permute-start | bytes 786440 | tf_op jit(solution)/shard_map/while/body/eval_jaxpr/ppermute | solution.py:13
  163.0 1.1 collective-permute-done
  164.2 10.2 %collective-permute-start = (bf16[128,1024]{0,1:T(8,128)(2,1)S(1)}, bf16[128,1024]{0,1:T(8,128)(2,1)S(1)}, u32[]{:S(2)}, u32[]{:S(2)}) collective-permute-start(bf16[128,1024]{0,1:T(8,128)(2,1)S(1)} %get-tuple-element.850), channel_id=1, source_target_pairs={{0,1},{1,2},{2,3},{3,4},{4,5},{5,6},{6,7},{8,9},{9,10},{10,11},{11... | collective-permute-start | bytes 786440 | tf_op jit(solution)/shard_map/while/body/eval_jaxpr/ppermute | solution.py:13
  174.3 1.1 collective-permute-done
  175.5 6.6 %collective-permute-start = (bf16[128,1024]{0,1:T(8,128)(2,1)S(1)}, bf16[128,1024]{0,1:T(8,128)(2,1)S(1)}, u32[]{:S(2)}, u32[]{:S(2)}) collective-permute-start(bf16[128,1024]{0,1:T(8,128)(2,1)S(1)} %get-tuple-element.850), channel_id=1, source_target_pairs={{0,1},{1,2},{2,3},{3,4},{4,5},{5,6},{6,7},{8,9},{9,10},{10,11},{11... | collective-permute-start | bytes 786440 | tf_op jit(solution)/shard_map/while/body/eval_jaxpr/ppermute | solution.py:13
  182.1 1.1 collective-permute-done
  183.2 5.4 %copy.108 = f32[4,2048,128]{1,2,0:T(8,128)} copy(f32[4,2048,128]{2,1,0:T(8,128)} %get-tuple-element.456) | data formatting | bytes 8388608 | tf_op jit(solution)/shard_map/while | solution.py:152
  188.7 5.0 %multiply_reduce_fusion = (f32[4,2048]{1,0:T(4,128)S(1)}, bf16[4,2048,128]{1,2,0:T(8,128)(2,1)}) fusion(bf16[4,2048,128]{1,2,0:T(8,128)(2,1)} %reshape.240, f32[4,2048,128]{1,2,0:T(8,128)} %copy.108, f32[4,2048]{1,0:T(4,128)S(1)} %bitcast.152), kind=kLoop, calls=%fused_computation.44 | loop fusion | flops 6283264 | bytes 8454144 | tf_op jit(solution)/shard_map/reduce_sum | solution.py:158
  193.7 2.2 broadcast.182
  195.9 169.3 %while.39 = (s32[]{:T(128)}, f32[128,1024]{0,1:T(8,128)S(1)}, f32[4,2048,128]{2,1,0:T(8,128)}, s32[]{:T(128)}, bf16[8,128,1024]{1,2,0:T(8,128)(2,1)}, /*index=5*...) while((s32[]{:T(128)}, f32[128,1024]{0,1:T(8,128)S(1)}, ...), condition=%wide.region_12.13_spmd.clone, body=%wide.region_9.12_spmd.clone.sunk | while | flops 1351823360 | bytes 85468640 | solution.py:212
  196.0 10.5 %conditional.7 = ((f32[128,1024]{0,1:T(8,128)S(1)}, f32[4,2048,128]{2,1,0:T(8,128)})) conditional(s32[]{:T(128)} %convert_element_type.142, (f32[128,1024]{0,1:T(8,128)S(1)}, f32[4,2048,128]{2,1,0:T(8,128)}) %tuple.112, (s32[]{:T(128)}, s32[]{:T(128)}, s32[2048]{0:T(1024)S(1)}, s32[128]{0:T(128)S(1)}, bf16[8,128,1024]{1,2,0:T(8,128)(2,1)}, ...), branch_computations={%region_10.10_spmd, %region_11.11_spmd.clone} | conditional | flops 1351428096 | bytes 81781416 | solution.py:208
  196.0 1.0 dynamic-slice_bitcast_fusion
  197.3 1.4 bitcast_select_fusion
  201.0 1.3 copy-done.3
  202.4 2.2 convolution_add_fusion
  204.6 1.9 copy-done.4
  206.5 14.3 %collective-permute-start.1 = (bf16[128,1024]{0,1:T(8,128)(2,1)S(1)}, bf16[128,1024]{0,1:T(8,128)(2,1)S(1)}, u32[]{:S(2)}, u32[]{:S(2)}) collective-permute-start(bf16[128,1024]{0,1:T(8,128)(2,1)S(1)} %convert_element_type.143), channel_id=1, source_target_pairs={{0,1},{1,2},{2,3},{3,4},{4,5},{5,6},{6,7},{7,0},{8,9},{9,10},{10,1... | collective-permute-start | bytes 786440 | tf_op jit(solution)/shard_map/while/body/eval_jaxpr/ppermute | solution.py:19
  220.9 37.2 %collective-permute-done.1 = bf16[128,1024]{0,1:T(8,128)(2,1)S(1)} collective-permute-done((bf16[128,1024]{0,1:T(8,128)(2,1)S(1)}, bf16[128,1024]{0,1:T(8,128)(2,1)S(1)}, u32[]{:S(2)}, u32[]{:S(2)}) %collective-permute-start.1) | collective-permute-done | bytes 262176 | tf_op jit(solution)/shard_map/while/body/eval_jaxpr/ppermute | solution.py:19
  258.3 13.8 %collective-permute-done.1 = bf16[128,1024]{0,1:T(8,128)(2,1)S(1)} collective-permute-done((bf16[128,1024]{0,1:T(8,128)(2,1)S(1)}, bf16[128,1024]{0,1:T(8,128)(2,1)S(1)}, u32[]{:S(2)}, u32[]{:S(2)}) %collective-permute-start.1) | collective-permute-done | bytes 262176 | tf_op jit(solution)/shard_map/while/body/eval_jaxpr/ppermute | solution.py:19
  272.4 13.8 %collective-permute-done.1 = bf16[128,1024]{0,1:T(8,128)(2,1)S(1)} collective-permute-done((bf16[128,1024]{0,1:T(8,128)(2,1)S(1)}, bf16[128,1024]{0,1:T(8,128)(2,1)S(1)}, u32[]{:S(2)}, u32[]{:S(2)}) %collective-permute-start.1) | collective-permute-done | bytes 262176 | tf_op jit(solution)/shard_map/while/body/eval_jaxpr/ppermute | solution.py:19
  286.5 13.8 %collective-permute-done.1 = bf16[128,1024]{0,1:T(8,128)(2,1)S(1)} collective-permute-done((bf16[128,1024]{0,1:T(8,128)(2,1)S(1)}, bf16[128,1024]{0,1:T(8,128)(2,1)S(1)}, u32[]{:S(2)}, u32[]{:S(2)}) %collective-permute-start.1) | collective-permute-done | bytes 262176 | tf_op jit(solution)/shard_map/while/body/eval_jaxpr/ppermute | solution.py:19
  300.6 14.8 %collective-permute-done.1 = bf16[128,1024]{0,1:T(8,128)(2,1)S(1)} collective-permute-done((bf16[128,1024]{0,1:T(8,128)(2,1)S(1)}, bf16[128,1024]{0,1:T(8,128)(2,1)S(1)}, u32[]{:S(2)}, u32[]{:S(2)}) %collective-permute-start.1) | collective-permute-done | bytes 262176 | tf_op jit(solution)/shard_map/while/body/eval_jaxpr/ppermute | solution.py:19
  315.7 16.3 %collective-permute-done.1 = bf16[128,1024]{0,1:T(8,128)(2,1)S(1)} collective-permute-done((bf16[128,1024]{0,1:T(8,128)(2,1)S(1)}, bf16[128,1024]{0,1:T(8,128)(2,1)S(1)}, u32[]{:S(2)}, u32[]{:S(2)}) %collective-permute-start.1) | collective-permute-done | bytes 262176 | tf_op jit(solution)/shard_map/while/body/eval_jaxpr/ppermute | solution.py:19
  332.3 16.3 %collective-permute-done.1 = bf16[128,1024]{0,1:T(8,128)(2,1)S(1)} collective-permute-done((bf16[128,1024]{0,1:T(8,128)(2,1)S(1)}, bf16[128,1024]{0,1:T(8,128)(2,1)S(1)}, u32[]{:S(2)}, u32[]{:S(2)}) %collective-permute-start.1) | collective-permute-done | bytes 262176 | tf_op jit(solution)/shard_map/while/body/eval_jaxpr/ppermute | solution.py:19
  348.9 16.3 %collective-permute-done.1 = bf16[128,1024]{0,1:T(8,128)(2,1)S(1)} collective-permute-done((bf16[128,1024]{0,1:T(8,128)(2,1)S(1)}, bf16[128,1024]{0,1:T(8,128)(2,1)S(1)}, u32[]{:S(2)}, u32[]{:S(2)}) %collective-permute-start.1) | collective-permute-done | bytes 262176 | tf_op jit(solution)/shard_map/while/body/eval_jaxpr/ppermute | solution.py:19
  366.4 5.6 %convert_bitcast_fusion = bf16[4096,1024]{0,1:T(8,128)(2,1)} fusion(bf16[128,4096]{0,1:T(8,128)(2,1)S(1)} %bitcast.151, bf16[128,512]{0,1:T(8,128)(2,1)S(1)} %slice.61, bf16[128,512]{0,1:T(8,128)(2,1)S(1)} %bitcast.158), kind=kOutput, calls=%fused_computation.39 | convolution fusion | flops 1078460416 | bytes 9699328 | tf_op jit(solution)/shard_map/dot_general | solution.py:229
  372.1 86.9 %reduce-scatter.5.cloned.1.call-done = bf16[512,1024]{0,1:T(8,128)(2,1)} async-done(((bf16[4096,1024]{0,1:T(8,128)(2,1)}), bf16[512,1024]{0,1:T(8,128)(2,1)}) %reduce-scatter.5.cloned.1.call-update) | async-done | bytes 1048592 | tf_op jit(solution)/shard_map/reduce_scatter | solution.py:228
  458.9 2.3 copy.131
  461.3 2.2 copy.140
  463.5 3.8 copy.109
  467.2 4.2 broadcast_in_dim_reshape.3
  471.4 2.8 multiply_convert_fusion
  474.2 1.4 copy.152
  475.6 2.3 convert_element_type.107
  477.9 7.3 %fusion.22 = bf16[1,128,4096]{2,1,0:T(8,128)(2,1)} fusion(bf16[4096,1024]{1,0:T(8,128)(2,1)} %all-gather.2.cloned.1.call-done, bf16[128,512]{0,1:T(8,128)(2,1)S(1)} %slice.61, bf16[128,512]{0,1:T(8,128)(2,1)S(1)} %bitcast.159), kind=kOutput, calls=%fused_computation.41 | convolution fusion | flops 1074790400 | bytes 9699328 | tf_op jit(solution)/shard_map/dot_general | solution.py:220
  485.1 3.2 reduce-scatter.7.cloned.1.call-done
  488.3 1.1 copy.132
  (155 shorter events, 11.1 us)
Async XLA Ops:
  7.2 83.6 %all-gather.2.cloned.1.call-start = ((), (), s32[]{:S(2)}) async-start(), calls=%async_computation.2 | async-start | bytes 8650752 | tf_op jit(solution)/shard_map/all_gather | solution.py:67
  7.9 451.1 %reduce-scatter.5.cloned.1.call-start = ((), (), s32[]{:S(2)}) async-start(), calls=%async_computation.3 | async-start | bytes 9437184 | tf_op jit(solution)/shard_map/reduce_scatter | solution.py:228
  34.3 64.1 %copy-start.8 = (f32[128,64]{1,0:T(8,128)}, f32[128,64]{1,0:T(8,128)S(1)}, u32[]{:S(2)}) copy-start(f32[128,64]{1,0:T(8,128)S(1)} %get-tuple-element.707) | copy-start | bytes 98308
  34.3 64.1 %copy-start.10 = (f32[128,64]{1,0:T(8,128)}, f32[128,64]{1,0:T(8,128)S(1)}, u32[]{:S(2)}) copy-start(f32[128,64]{1,0:T(8,128)S(1)} %get-tuple-element.708) | copy-start | bytes 98308
  106.7 3.6 copy-start.7
  106.7 5.0 copy-start.12
  110.4 1.3 copy-start.5
  111.7 3.3 collective-permute-start
  115.0 16.2 %collective-permute-start = (bf16[128,1024]{0,1:T(8,128)(2,1)S(1)}, bf16[128,1024]{0,1:T(8,128)(2,1)S(1)}, u32[]{:S(2)}, u32[]{:S(2)}) collective-permute-start(bf16[128,1024]{0,1:T(8,128)(2,1)S(1)} %get-tuple-element.850), channel_id=1, source_target_pairs={{0,1},{1,2},{2,3},{3,4},{4,5},{5,6},{6,7},{8,9},{9,10},{10,11},{11... | collective-permute-start | bytes 786440 | tf_op jit(solution)/shard_map/while/body/eval_jaxpr/ppermute | solution.py:13
  131.3 7.7 %collective-permute-start = (bf16[128,1024]{0,1:T(8,128)(2,1)S(1)}, bf16[128,1024]{0,1:T(8,128)(2,1)S(1)}, u32[]{:S(2)}, u32[]{:S(2)}) collective-permute-start(bf16[128,1024]{0,1:T(8,128)(2,1)S(1)} %get-tuple-element.850), channel_id=1, source_target_pairs={{0,1},{1,2},{2,3},{3,4},{4,5},{5,6},{6,7},{8,9},{9,10},{10,11},{11... | collective-permute-start | bytes 786440 | tf_op jit(solution)/shard_map/while/body/eval_jaxpr/ppermute | solution.py:13
  139.0 17.3 %collective-permute-start = (bf16[128,1024]{0,1:T(8,128)(2,1)S(1)}, bf16[128,1024]{0,1:T(8,128)(2,1)S(1)}, u32[]{:S(2)}, u32[]{:S(2)}) collective-permute-start(bf16[128,1024]{0,1:T(8,128)(2,1)S(1)} %get-tuple-element.850), channel_id=1, source_target_pairs={{0,1},{1,2},{2,3},{3,4},{4,5},{5,6},{6,7},{8,9},{9,10},{10,11},{11... | collective-permute-start | bytes 786440 | tf_op jit(solution)/shard_map/while/body/eval_jaxpr/ppermute | solution.py:13
  156.4 7.7 %collective-permute-start = (bf16[128,1024]{0,1:T(8,128)(2,1)S(1)}, bf16[128,1024]{0,1:T(8,128)(2,1)S(1)}, u32[]{:S(2)}, u32[]{:S(2)}) collective-permute-start(bf16[128,1024]{0,1:T(8,128)(2,1)S(1)} %get-tuple-element.850), channel_id=1, source_target_pairs={{0,1},{1,2},{2,3},{3,4},{4,5},{5,6},{6,7},{8,9},{9,10},{10,11},{11... | collective-permute-start | bytes 786440 | tf_op jit(solution)/shard_map/while/body/eval_jaxpr/ppermute | solution.py:13
  164.2 11.3 %collective-permute-start = (bf16[128,1024]{0,1:T(8,128)(2,1)S(1)}, bf16[128,1024]{0,1:T(8,128)(2,1)S(1)}, u32[]{:S(2)}, u32[]{:S(2)}) collective-permute-start(bf16[128,1024]{0,1:T(8,128)(2,1)S(1)} %get-tuple-element.850), channel_id=1, source_target_pairs={{0,1},{1,2},{2,3},{3,4},{4,5},{5,6},{6,7},{8,9},{9,10},{10,11},{11... | collective-permute-start | bytes 786440 | tf_op jit(solution)/shard_map/while/body/eval_jaxpr/ppermute | solution.py:13
  175.5 7.7 %collective-permute-start = (bf16[128,1024]{0,1:T(8,128)(2,1)S(1)}, bf16[128,1024]{0,1:T(8,128)(2,1)S(1)}, u32[]{:S(2)}, u32[]{:S(2)}) collective-permute-start(bf16[128,1024]{0,1:T(8,128)(2,1)S(1)} %get-tuple-element.850), channel_id=1, source_target_pairs={{0,1},{1,2},{2,3},{3,4},{4,5},{5,6},{6,7},{8,9},{9,10},{10,11},{11... | collective-permute-start | bytes 786440 | tf_op jit(solution)/shard_map/while/body/eval_jaxpr/ppermute | solution.py:13
  195.9 169.7 %copy-start.9 = (f32[128,64]{1,0:T(8,128)S(1)}, f32[128,64]{1,0:T(8,128)}, u32[]{:S(2)}) copy-start(f32[128,64]{1,0:T(8,128)} %copy-done.8) | copy-start | bytes 98308
  195.9 169.7 %copy-start.11 = (f32[128,64]{1,0:T(8,128)S(1)}, f32[128,64]{1,0:T(8,128)}, u32[]{:S(2)}) copy-start(f32[128,64]{1,0:T(8,128)} %copy-done.10) | copy-start | bytes 98308
  197.0 1.7 copy-start
  200.2 2.2 copy-start.3
  204.6 1.9 copy-start.4
  206.5 51.5 %collective-permute-start.1 = (bf16[128,1024]{0,1:T(8,128)(2,1)S(1)}, bf16[128,1024]{0,1:T(8,128)(2,1)S(1)}, u32[]{:S(2)}, u32[]{:S(2)}) collective-permute-start(bf16[128,1024]{0,1:T(8,128)(2,1)S(1)} %convert_element_type.143), channel_id=1, source_target_pairs={{0,1},{1,2},{2,3},{3,4},{4,5},{5,6},{6,7},{7,0},{8,9},{9,10},{10,1... | collective-permute-start | bytes 786440 | tf_op jit(solution)/shard_map/while/body/eval_jaxpr/ppermute | solution.py:19
  258.3 13.9 %collective-permute-start.1 = (bf16[128,1024]{0,1:T(8,128)(2,1)S(1)}, bf16[128,1024]{0,1:T(8,128)(2,1)S(1)}, u32[]{:S(2)}, u32[]{:S(2)}) collective-permute-start(bf16[128,1024]{0,1:T(8,128)(2,1)S(1)} %convert_element_type.143), channel_id=1, source_target_pairs={{0,1},{1,2},{2,3},{3,4},{4,5},{5,6},{6,7},{7,0},{8,9},{9,10},{10,1... | collective-permute-start | bytes 786440 | tf_op jit(solution)/shard_map/while/body/eval_jaxpr/ppermute | solution.py:19
  272.4 13.9 %collective-permute-start.1 = (bf16[128,1024]{0,1:T(8,128)(2,1)S(1)}, bf16[128,1024]{0,1:T(8,128)(2,1)S(1)}, u32[]{:S(2)}, u32[]{:S(2)}) collective-permute-start(bf16[128,1024]{0,1:T(8,128)(2,1)S(1)} %convert_element_type.143), channel_id=1, source_target_pairs={{0,1},{1,2},{2,3},{3,4},{4,5},{5,6},{6,7},{7,0},{8,9},{9,10},{10,1... | collective-permute-start | bytes 786440 | tf_op jit(solution)/shard_map/while/body/eval_jaxpr/ppermute | solution.py:19
  286.5 13.9 %collective-permute-start.1 = (bf16[128,1024]{0,1:T(8,128)(2,1)S(1)}, bf16[128,1024]{0,1:T(8,128)(2,1)S(1)}, u32[]{:S(2)}, u32[]{:S(2)}) collective-permute-start(bf16[128,1024]{0,1:T(8,128)(2,1)S(1)} %convert_element_type.143), channel_id=1, source_target_pairs={{0,1},{1,2},{2,3},{3,4},{4,5},{5,6},{6,7},{7,0},{8,9},{9,10},{10,1... | collective-permute-start | bytes 786440 | tf_op jit(solution)/shard_map/while/body/eval_jaxpr/ppermute | solution.py:19
  300.5 14.9 %collective-permute-start.1 = (bf16[128,1024]{0,1:T(8,128)(2,1)S(1)}, bf16[128,1024]{0,1:T(8,128)(2,1)S(1)}, u32[]{:S(2)}, u32[]{:S(2)}) collective-permute-start(bf16[128,1024]{0,1:T(8,128)(2,1)S(1)} %convert_element_type.143), channel_id=1, source_target_pairs={{0,1},{1,2},{2,3},{3,4},{4,5},{5,6},{6,7},{7,0},{8,9},{9,10},{10,1... | collective-permute-start | bytes 786440 | tf_op jit(solution)/shard_map/while/body/eval_jaxpr/ppermute | solution.py:19
  315.7 16.4 %collective-permute-start.1 = (bf16[128,1024]{0,1:T(8,128)(2,1)S(1)}, bf16[128,1024]{0,1:T(8,128)(2,1)S(1)}, u32[]{:S(2)}, u32[]{:S(2)}) collective-permute-start(bf16[128,1024]{0,1:T(8,128)(2,1)S(1)} %convert_element_type.143), channel_id=1, source_target_pairs={{0,1},{1,2},{2,3},{3,4},{4,5},{5,6},{6,7},{7,0},{8,9},{9,10},{10,1... | collective-permute-start | bytes 786440 | tf_op jit(solution)/shard_map/while/body/eval_jaxpr/ppermute | solution.py:19
  332.2 16.4 %collective-permute-start.1 = (bf16[128,1024]{0,1:T(8,128)(2,1)S(1)}, bf16[128,1024]{0,1:T(8,128)(2,1)S(1)}, u32[]{:S(2)}, u32[]{:S(2)}) collective-permute-start(bf16[128,1024]{0,1:T(8,128)(2,1)S(1)} %convert_element_type.143), channel_id=1, source_target_pairs={{0,1},{1,2},{2,3},{3,4},{4,5},{5,6},{6,7},{7,0},{8,9},{9,10},{10,1... | collective-permute-start | bytes 786440 | tf_op jit(solution)/shard_map/while/body/eval_jaxpr/ppermute | solution.py:19
  348.8 16.4 %collective-permute-start.1 = (bf16[128,1024]{0,1:T(8,128)(2,1)S(1)}, bf16[128,1024]{0,1:T(8,128)(2,1)S(1)}, u32[]{:S(2)}, u32[]{:S(2)}) collective-permute-start(bf16[128,1024]{0,1:T(8,128)(2,1)S(1)} %convert_element_type.143), channel_id=1, source_target_pairs={{0,1},{1,2},{2,3},{3,4},{4,5},{5,6},{6,7},{7,0},{8,9},{9,10},{10,1... | collective-permute-start | bytes 786440 | tf_op jit(solution)/shard_map/while/body/eval_jaxpr/ppermute | solution.py:19
  365.2 1.2 copy-start.6
  372.0 116.3 %reduce-scatter.7.cloned.1.call-start = ((), (), s32[]{:S(2)}) async-start(), calls=%async_computation.4 | async-start | bytes 1310720
Sparse Core Ops, SparseCore 0:
  11.0 79.7 all-gather.1
  372.2 86.7 reduce-scatter.4
  461.8 26.4 reduce-scatter.6
where the time goes:
time: 498 us; the launch traced here: 497 us
  waiting for transfers between devices  297 us (60%)
  starting transfers between devices  78.1 us (16%)
  local copies, waits for them, and re-layouts  65 us (13%)
  matrix products  29 us (6%)
  between operations  14 us (3%)
  other arithmetic  13.1 us (3%)
    ppermute x8, waiting for transfers between devices, shifted_2(): return lax.ppermute(value, axis, pairs)  142 us
    reduce_scatter x1, waiting for transfers between devices, on_device(): lax.psum_scatter(lax.dot_general(reordered, grad_projected, (((0,), (0,))...  86.9 us
    ppermute x7, starting transfers between devices, shifted(): return lax.ppermute(block, axis, route)  63.3 us
    all_gather x1, waiting for transfers between devices, on_device(): weight_all = lax.all_gather(kv_weight, ('dp', 'ctx'), axis=0, tiled=True)  55.6 us
    unnamed x27, local copies, waits for them, and re-layouts  20.9 us
    ppermute x8, starting transfers between devices, shifted_2(): return lax.ppermute(value, axis, pairs)  14.7 us
  transfers between devices with their start and end apart: 18, of which 18 were waited for; matrix products, arithmetic and copies ran while one was open for 10% of the time, Pallas kernels for 0%

commit v1 on v0

--- a/solution.py
+++ b/solution.py
@@ -64,7 +64,15 @@
     score_scale = head_dim ** (-0.5)
     shard_rows = model_width // (data_size * ctx_size)
     tokens = inputs[0]
-    weight_all = lax.all_gather(kv_weight, ("dp", "ctx"), axis=0, tiled=True)
+
+    def roads_pass(raw):
+        pile = []
+        for _ in range(jax.lax.axis_size(("dp", "ctx"))):
+            pile.append(raw)
+        back = jax.lax.all_to_all(jnp.stack(pile, axis=0), ("dp", "ctx"), 0, 0)
+        return jnp.concatenate(back, axis=0)
+
+    weight_all = roads_pass(kv_weight)
     projected = jnp.dot(tokens, weight_all, preferred_element_type=jnp.float32)
     positions = ctx_index * token_count + jnp.arange(token_count, dtype=jnp.int32)
     key_rows = rotary(

time: 498 us -> 612 us (1.23)
  waiting for transfers between devices: 297 us -> 399 us
  local copies, waits for them, and re-layouts: 65 us -> 71.8 us
    all_to_all x0 -> x1, waiting for transfers between devices: none -> 159 us  [roads_pass(): back = jax.lax.all_to_all(jnp.stack(pile, axis=0), ('dp', 'ctx'), 0, 0)]
    all_gather x1 -> x0, waiting for transfers between devices: 55.6 us -> none  [on_device(): weight_all = lax.all_gather(kv_weight, ('dp', 'ctx'), axis=0, tiled=True)]
    all_to_all x0 -> x1, starting transfers between devices: none -> 7.45 us  [roads_pass(): back = jax.lax.all_to_all(jnp.stack(pile, axis=0), ('dp', 'ctx'), 0, 0)]
    unnamed x27 -> x29, local copies, waits for them, and re-layouts: 20.9 us -> 19.3 us
  transfers between devices with their start and end apart: 18 -> 18, of which waited for: 18 -> 17; matrix products, arithmetic and copies ran while one was open for 10% -> 9% of each run, Pallas kernels for 0% -> 0%
where the time goes in v1:
time: 612 us; the launch traced here: 610 us
  waiting for transfers between devices  399 us (65%)
  starting transfers between devices  82 us (13%)
  local copies, waits for them, and re-layouts  71.8 us (12%)
  matrix products  29.1 us (5%)
  between operations  14.4 us (2%)
  other arithmetic  13 us (2%)
    all_to_all x1, waiting for transfers between devices, roads_pass(): back = jax.lax.all_to_all(jnp.stack(pile, axis=0), ('dp', 'ctx'), 0, 0)  159 us
    ppermute x8, waiting for transfers between devices, shifted_2(): return lax.ppermute(value, axis, pairs)  144 us
    reduce_scatter x1, waiting for transfers between devices, on_device(): lax.psum_scatter(lax.dot_general(reordered, grad_projected, (((0,), (0,))...  87.9 us
    ppermute x7, starting transfers between devices, shifted(): return lax.ppermute(block, axis, route)  59.7 us
    unnamed x29, local copies, waits for them, and re-layouts  19.3 us
    ppermute x8, starting transfers between devices, shifted_2(): return lax.ppermute(value, axis, pairs)  14.7 us
  transfers between devices with their start and end apart: 18, of which 17 were waited for; matrix products, arithmetic and copies ran while one was open for 9% of the time, Pallas kernels for 0%

profile of v1, /device:TPU:0, one launch (start us, length us, event | category | flops | bytes accessed | tf_op | source)
XLA Modules:
  0.0 610.4 jit_solution(12476870145067675085)
XLA Ops:
  7.2 5.2 stack.2
  12.4 7.5 %all-to-all-start = ((bf16[32,128,1024]{2,1,0:T(8,128)(2,1)}), bf16[32,128,1024]{2,1,0:T(8,128)(2,1)}, u32[]{:S(2)}, u32[]{:S(2)}) async-start(bf16[32,128,1024]{2,1,0:T(8,128)(2,1)} %stack.2), calls=%async_computation | async-start | bytes 16777216 | tf_op jit(solution)/shard_map/all_to_all | solution.py:72
  19.9 1.9 copy.141
  21.9 4.3 copy.110
  26.1 2.3 reshape.246
  28.4 2.2 copy.139
  30.6 3.8 copy.102
  34.4 2.8 reshape.243
  37.3 2.5 copy.107
  39.7 2.3 copy.115
  42.0 2.3 copy.116
  45.5 159.1 %all-to-all-done = bf16[32,128,1024]{2,1,0:T(8,128)(2,1)} async-done(((bf16[32,128,1024]{2,1,0:T(8,128)(2,1)}), bf16[32,128,1024]{2,1,0:T(8,128)(2,1)}, u32[]{:S(2)}, u32[]{:S(2)}) %all-to-all-start) | async-done | bytes 8388640 | tf_op jit(solution)/shard_map/all_to_all | solution.py:72
  204.7 5.0 fusion.27
  211.0 1.0 reshape.242
  212.5 1.8 fusion.36
  214.2 1.8 copy.106
  216.0 1.8 copy.101
  217.8 2.1 fusion.41
  220.6 3.3 convolution_add_fusion.1
  224.3 1.3 copy-done.5
  225.6 68.0 %while.38 = (s32[]{:T(128)}, bf16[128,1024]{0,1:T(8,128)(2,1)S(1)}, bf16[8,128,1024]{1,2,0:T(8,128)(2,1)}, f32[4,2048,1]{1,0,2:T(4,128)S(1)}, f32[4,2048,1]{1,0,...) while((s32[]{:T(128)}, bf16[128,1024]{0,1:T(8,128)(2,1)S(1)}, ...), condition=%wide.region_7.8_spmd.clone, body=%wide.region_2.7_spmd.clone.sunk | while | flops 551063552 | bytes 61154760 | solution.py:160
  225.6 1.7 collective-permute-start
  227.3 1.1 collective-permute-done
  228.4 13.7 %collective-permute-start = (bf16[128,1024]{0,1:T(8,128)(2,1)S(1)}, bf16[128,1024]{0,1:T(8,128)(2,1)S(1)}, u32[]{:S(2)}, u32[]{:S(2)}) collective-permute-start(bf16[128,1024]{0,1:T(8,128)(2,1)S(1)} %get-tuple-element.850), channel_id=1, source_target_pairs={{0,1},{1,2},{2,3},{3,4},{4,5},{5,6},{6,7},{8,9},{9,10},{10,11},{11... | collective-permute-start | bytes 786440 | tf_op jit(solution)/shard_map/while/body/eval_jaxpr/ppermute | solution.py:13
  242.2 1.1 collective-permute-done
  243.4 6.6 %collective-permute-start = (bf16[128,1024]{0,1:T(8,128)(2,1)S(1)}, bf16[128,1024]{0,1:T(8,128)(2,1)S(1)}, u32[]{:S(2)}, u32[]{:S(2)}) collective-permute-start(bf16[128,1024]{0,1:T(8,128)(2,1)S(1)} %get-tuple-element.850), channel_id=1, source_target_pairs={{0,1},{1,2},{2,3},{3,4},{4,5},{5,6},{6,7},{8,9},{9,10},{10,11},{11... | collective-permute-start | bytes 786440 | tf_op jit(solution)/shard_map/while/body/eval_jaxpr/ppermute | solution.py:13
  249.9 1.1 collective-permute-done
  251.1 16.2 %collective-permute-start = (bf16[128,1024]{0,1:T(8,128)(2,1)S(1)}, bf16[128,1024]{0,1:T(8,128)(2,1)S(1)}, u32[]{:S(2)}, u32[]{:S(2)}) collective-permute-start(bf16[128,1024]{0,1:T(8,128)(2,1)S(1)} %get-tuple-element.850), channel_id=1, source_target_pairs={{0,1},{1,2},{2,3},{3,4},{4,5},{5,6},{6,7},{8,9},{9,10},{10,11},{11... | collective-permute-start | bytes 786440 | tf_op jit(solution)/shard_map/while/body/eval_jaxpr/ppermute | solution.py:13
  267.3 1.1 collective-permute-done
  268.5 6.6 %collective-permute-start = (bf16[128,1024]{0,1:T(8,128)(2,1)S(1)}, bf16[128,1024]{0,1:T(8,128)(2,1)S(1)}, u32[]{:S(2)}, u32[]{:S(2)}) collective-permute-start(bf16[128,1024]{0,1:T(8,128)(2,1)S(1)} %get-tuple-element.850), channel_id=1, source_target_pairs={{0,1},{1,2},{2,3},{3,4},{4,5},{5,6},{6,7},{8,9},{9,10},{10,11},{11... | collective-permute-start | bytes 786440 | tf_op jit(solution)/shard_map/while/body/eval_jaxpr/ppermute | solution.py:13
  275.1 1.1 collective-permute-done
  276.2 8.5 %collective-permute-start = (bf16[128,1024]{0,1:T(8,128)(2,1)S(1)}, bf16[128,1024]{0,1:T(8,128)(2,1)S(1)}, u32[]{:S(2)}, u32[]{:S(2)}) collective-permute-start(bf16[128,1024]{0,1:T(8,128)(2,1)S(1)} %get-tuple-element.850), channel_id=1, source_target_pairs={{0,1},{1,2},{2,3},{3,4},{4,5},{5,6},{6,7},{8,9},{9,10},{10,11},{11... | collective-permute-start | bytes 786440 | tf_op jit(solution)/shard_map/while/body/eval_jaxpr/ppermute | solution.py:13
  284.7 1.1 collective-permute-done
  285.8 6.6 %collective-permute-start = (bf16[128,1024]{0,1:T(8,128)(2,1)S(1)}, bf16[128,1024]{0,1:T(8,128)(2,1)S(1)}, u32[]{:S(2)}, u32[]{:S(2)}) collective-permute-start(bf16[128,1024]{0,1:T(8,128)(2,1)S(1)} %get-tuple-element.850), channel_id=1, source_target_pairs={{0,1},{1,2},{2,3},{3,4},{4,5},{5,6},{6,7},{8,9},{9,10},{10,11},{11... | collective-permute-start | bytes 786440 | tf_op jit(solution)/shard_map/while/body/eval_jaxpr/ppermute | solution.py:13
  292.4 1.1 collective-permute-done
  293.6 5.4 copy.108
  299.0 5.0 multiply_reduce_fusion
  304.0 2.2 broadcast.184
  306.2 170.9 %while.39 = (s32[]{:T(128)}, f32[128,1024]{0,1:T(8,128)S(1)}, f32[4,2048,128]{2,1,0:T(8,128)}, s32[]{:T(128)}, bf16[8,128,1024]{1,2,0:T(8,128)(2,1)}, /*index=5*...) while((s32[]{:T(128)}, f32[128,1024]{0,1:T(8,128)S(1)}, ...), condition=%wide.region_12.13_spmd.clone, body=%wide.region_9.12_spmd.clone.sunk | while | flops 1351823360 | bytes 85468640 | solution.py:220
  306.3 10.6 %conditional.7 = ((f32[128,1024]{0,1:T(8,128)S(1)}, f32[4,2048,128]{2,1,0:T(8,128)})) conditional(s32[]{:T(128)} %convert_element_type.142, (f32[128,1024]{0,1:T(8,128)S(1)}, f32[4,2048,128]{2,1,0:T(8,128)}) %tuple.112, (s32[]{:T(128)}, s32[]{:T(128)}, s32[2048]{0:T(1024)S(1)}, s32[128]{0:T(128)S(1)}, bf16[8,128,1024]{1,2,0:T(8,128)(2,1)}, ...), branch_computations={%region_10.10_spmd, %region_11.11_spmd.clone} | conditional | flops 1351428096 | bytes 81781416 | solution.py:216
  307.6 1.4 bitcast_select_fusion
  311.4 1.3 copy-done.3
  312.7 2.2 convolution_add_fusion
  314.9 1.9 copy-done.4
  316.9 14.3 %collective-permute-start.1 = (bf16[128,1024]{0,1:T(8,128)(2,1)S(1)}, bf16[128,1024]{0,1:T(8,128)(2,1)S(1)}, u32[]{:S(2)}, u32[]{:S(2)}) collective-permute-start(bf16[128,1024]{0,1:T(8,128)(2,1)S(1)} %convert_element_type.143), channel_id=1, source_target_pairs={{0,1},{1,2},{2,3},{3,4},{4,5},{5,6},{6,7},{7,0},{8,9},{9,10},{10,1... | collective-permute-start | bytes 786440 | tf_op jit(solution)/shard_map/while/body/eval_jaxpr/ppermute | solution.py:19
  331.2 38.8 %collective-permute-done.1 = bf16[128,1024]{0,1:T(8,128)(2,1)S(1)} collective-permute-done((bf16[128,1024]{0,1:T(8,128)(2,1)S(1)}, bf16[128,1024]{0,1:T(8,128)(2,1)S(1)}, u32[]{:S(2)}, u32[]{:S(2)}) %collective-permute-start.1) | collective-permute-done | bytes 262176 | tf_op jit(solution)/shard_map/while/body/eval_jaxpr/ppermute | solution.py:19
  370.2 13.8 %collective-permute-done.1 = bf16[128,1024]{0,1:T(8,128)(2,1)S(1)} collective-permute-done((bf16[128,1024]{0,1:T(8,128)(2,1)S(1)}, bf16[128,1024]{0,1:T(8,128)(2,1)S(1)}, u32[]{:S(2)}, u32[]{:S(2)}) %collective-permute-start.1) | collective-permute-done | bytes 262176 | tf_op jit(solution)/shard_map/while/body/eval_jaxpr/ppermute | solution.py:19
  384.3 13.8 %collective-permute-done.1 = bf16[128,1024]{0,1:T(8,128)(2,1)S(1)} collective-permute-done((bf16[128,1024]{0,1:T(8,128)(2,1)S(1)}, bf16[128,1024]{0,1:T(8,128)(2,1)S(1)}, u32[]{:S(2)}, u32[]{:S(2)}) %collective-permute-start.1) | collective-permute-done | bytes 262176 | tf_op jit(solution)/shard_map/while/body/eval_jaxpr/ppermute | solution.py:19
  398.4 13.8 %collective-permute-done.1 = bf16[128,1024]{0,1:T(8,128)(2,1)S(1)} collective-permute-done((bf16[128,1024]{0,1:T(8,128)(2,1)S(1)}, bf16[128,1024]{0,1:T(8,128)(2,1)S(1)}, u32[]{:S(2)}, u32[]{:S(2)}) %collective-permute-start.1) | collective-permute-done | bytes 262176 | tf_op jit(solution)/shard_map/while/body/eval_jaxpr/ppermute | solution.py:19
  412.5 14.8 %collective-permute-done.1 = bf16[128,1024]{0,1:T(8,128)(2,1)S(1)} collective-permute-done((bf16[128,1024]{0,1:T(8,128)(2,1)S(1)}, bf16[128,1024]{0,1:T(8,128)(2,1)S(1)}, u32[]{:S(2)}, u32[]{:S(2)}) %collective-permute-start.1) | collective-permute-done | bytes 262176 | tf_op jit(solution)/shard_map/while/body/eval_jaxpr/ppermute | solution.py:19
  427.6 16.3 %collective-permute-done.1 = bf16[128,1024]{0,1:T(8,128)(2,1)S(1)} collective-permute-done((bf16[128,1024]{0,1:T(8,128)(2,1)S(1)}, bf16[128,1024]{0,1:T(8,128)(2,1)S(1)}, u32[]{:S(2)}, u32[]{:S(2)}) %collective-permute-start.1) | collective-permute-done | bytes 262176 | tf_op jit(solution)/shard_map/while/body/eval_jaxpr/ppermute | solution.py:19
  444.2 16.3 %collective-permute-done.1 = bf16[128,1024]{0,1:T(8,128)(2,1)S(1)} collective-permute-done((bf16[128,1024]{0,1:T(8,128)(2,1)S(1)}, bf16[128,1024]{0,1:T(8,128)(2,1)S(1)}, u32[]{:S(2)}, u32[]{:S(2)}) %collective-permute-start.1) | collective-permute-done | bytes 262176 | tf_op jit(solution)/shard_map/while/body/eval_jaxpr/ppermute | solution.py:19
  460.8 16.3 %collective-permute-done.1 = bf16[128,1024]{0,1:T(8,128)(2,1)S(1)} collective-permute-done((bf16[128,1024]{0,1:T(8,128)(2,1)S(1)}, bf16[128,1024]{0,1:T(8,128)(2,1)S(1)}, u32[]{:S(2)}, u32[]{:S(2)}) %collective-permute-start.1) | collective-permute-done | bytes 262176 | tf_op jit(solution)/shard_map/while/body/eval_jaxpr/ppermute | solution.py:19
  478.4 5.6 convert_bitcast_fusion
  484.0 87.9 %reduce-scatter.5.cloned.1.call-done = bf16[512,1024]{0,1:T(8,128)(2,1)} async-done(((bf16[4096,1024]{0,1:T(8,128)(2,1)}), bf16[512,1024]{0,1:T(8,128)(2,1)}) %reduce-scatter.5.cloned.1.call-update) | async-done | bytes 1048592 | tf_op jit(solution)/shard_map/reduce_scatter | solution.py:236
  571.9 2.3 copy.131
  574.2 2.2 copy.140
  576.4 3.8 copy.109
  580.2 4.2 broadcast_in_dim_reshape.3
  584.3 2.8 multiply_convert_fusion
  587.1 2.7 copy.152
  589.9 4.2 convert_element_type.107
  594.0 7.4 %fusion.22 = bf16[1,128,4096]{2,1,0:T(8,128)(2,1)} fusion(bf16[4096,1024]{1,0:T(8,128)(2,1)} %bitcast.19, bf16[128,512]{0,1:T(8,128)(2,1)S(1)} %slice.61, bf16[128,512]{0,1:T(8,128)(2,1)S(1)} %bitcast.160), kind=kOutput, calls=%fused_computation.41 | convolution fusion | flops 1074790400 | bytes 9699328 | tf_op jit(solution)/shard_map/dot_general | solution.py:228
  601.5 1.1 copy.132
  (157 shorter events, 11.3 us)
Async XLA Ops:
  12.4 7.5 %copy-start.7 = (bf16[1,128,8192]{2,1,0:T(8,128)(2,1)S(1)}, bf16[1,128,8192]{2,1,0:T(8,128)(2,1)}, u32[]{:S(2)}) copy-start(bf16[1,128,8192]{2,1,0:T(8,128)(2,1)} %param.14) | copy-start | bytes 6291460
  12.4 192.2 %all-to-all-start = ((bf16[32,128,1024]{2,1,0:T(8,128)(2,1)}), bf16[32,128,1024]{2,1,0:T(8,128)(2,1)}, u32[]{:S(2)}, u32[]{:S(2)}) async-start(bf16[32,128,1024]{2,1,0:T(8,128)(2,1)} %stack.2), calls=%async_computation | async-start | bytes 16777216 | tf_op jit(solution)/shard_map/all_to_all | solution.py:72
  19.9 552.0 %reduce-scatter.5.cloned.1.call-start = ((), (), s32[]{:S(2)}) async-start(), calls=%async_computation.3 | async-start | bytes 9437184 | tf_op jit(solution)/shard_map/reduce_scatter | solution.py:236
  44.6 167.6 %copy-start.9 = (f32[128,64]{1,0:T(8,128)}, f32[128,64]{1,0:T(8,128)S(1)}, u32[]{:S(2)}) copy-start(f32[128,64]{1,0:T(8,128)S(1)} %get-tuple-element.707) | copy-start | bytes 98308
  44.7 167.6 %copy-start.11 = (f32[128,64]{1,0:T(8,128)}, f32[128,64]{1,0:T(8,128)S(1)}, u32[]{:S(2)}) copy-start(f32[128,64]{1,0:T(8,128)S(1)} %get-tuple-element.708) | copy-start | bytes 98308
  220.6 3.6 copy-start.8
  220.6 5.0 copy-start.13
  224.3 1.3 copy-start.5
  225.6 2.8 collective-permute-start
  228.4 14.9 %collective-permute-start = (bf16[128,1024]{0,1:T(8,128)(2,1)S(1)}, bf16[128,1024]{0,1:T(8,128)(2,1)S(1)}, u32[]{:S(2)}, u32[]{:S(2)}) collective-permute-start(bf16[128,1024]{0,1:T(8,128)(2,1)S(1)} %get-tuple-element.850), channel_id=1, source_target_pairs={{0,1},{1,2},{2,3},{3,4},{4,5},{5,6},{6,7},{8,9},{9,10},{10,11},{11... | collective-permute-start | bytes 786440 | tf_op jit(solution)/shard_map/while/body/eval_jaxpr/ppermute | solution.py:13
  243.4 7.7 %collective-permute-start = (bf16[128,1024]{0,1:T(8,128)(2,1)S(1)}, bf16[128,1024]{0,1:T(8,128)(2,1)S(1)}, u32[]{:S(2)}, u32[]{:S(2)}) collective-permute-start(bf16[128,1024]{0,1:T(8,128)(2,1)S(1)} %get-tuple-element.850), channel_id=1, source_target_pairs={{0,1},{1,2},{2,3},{3,4},{4,5},{5,6},{6,7},{8,9},{9,10},{10,11},{11... | collective-permute-start | bytes 786440 | tf_op jit(solution)/shard_map/while/body/eval_jaxpr/ppermute | solution.py:13
  251.1 17.3 %collective-permute-start = (bf16[128,1024]{0,1:T(8,128)(2,1)S(1)}, bf16[128,1024]{0,1:T(8,128)(2,1)S(1)}, u32[]{:S(2)}, u32[]{:S(2)}) collective-permute-start(bf16[128,1024]{0,1:T(8,128)(2,1)S(1)} %get-tuple-element.850), channel_id=1, source_target_pairs={{0,1},{1,2},{2,3},{3,4},{4,5},{5,6},{6,7},{8,9},{9,10},{10,11},{11... | collective-permute-start | bytes 786440 | tf_op jit(solution)/shard_map/while/body/eval_jaxpr/ppermute | solution.py:13
  268.5 7.7 %collective-permute-start = (bf16[128,1024]{0,1:T(8,128)(2,1)S(1)}, bf16[128,1024]{0,1:T(8,128)(2,1)S(1)}, u32[]{:S(2)}, u32[]{:S(2)}) collective-permute-start(bf16[128,1024]{0,1:T(8,128)(2,1)S(1)} %get-tuple-element.850), channel_id=1, source_target_pairs={{0,1},{1,2},{2,3},{3,4},{4,5},{5,6},{6,7},{8,9},{9,10},{10,11},{11... | collective-permute-start | bytes 786440 | tf_op jit(solution)/shard_map/while/body/eval_jaxpr/ppermute | solution.py:13
  276.2 9.6 %collective-permute-start = (bf16[128,1024]{0,1:T(8,128)(2,1)S(1)}, bf16[128,1024]{0,1:T(8,128)(2,1)S(1)}, u32[]{:S(2)}, u32[]{:S(2)}) collective-permute-start(bf16[128,1024]{0,1:T(8,128)(2,1)S(1)} %get-tuple-element.850), channel_id=1, source_target_pairs={{0,1},{1,2},{2,3},{3,4},{4,5},{5,6},{6,7},{8,9},{9,10},{10,11},{11... | collective-permute-start | bytes 786440 | tf_op jit(solution)/shard_map/while/body/eval_jaxpr/ppermute | solution.py:13
  285.8 7.7 %collective-permute-start = (bf16[128,1024]{0,1:T(8,128)(2,1)S(1)}, bf16[128,1024]{0,1:T(8,128)(2,1)S(1)}, u32[]{:S(2)}, u32[]{:S(2)}) collective-permute-start(bf16[128,1024]{0,1:T(8,128)(2,1)S(1)} %get-tuple-element.850), channel_id=1, source_target_pairs={{0,1},{1,2},{2,3},{3,4},{4,5},{5,6},{6,7},{8,9},{9,10},{10,11},{11... | collective-permute-start | bytes 786440 | tf_op jit(solution)/shard_map/while/body/eval_jaxpr/ppermute | solution.py:13
  306.2 171.3 %copy-start.10 = (f32[128,64]{1,0:T(8,128)S(1)}, f32[128,64]{1,0:T(8,128)}, u32[]{:S(2)}) copy-start(f32[128,64]{1,0:T(8,128)} %copy-done.9) | copy-start | bytes 98308
  306.2 171.3 %copy-start.12 = (f32[128,64]{1,0:T(8,128)S(1)}, f32[128,64]{1,0:T(8,128)}, u32[]{:S(2)}) copy-start(f32[128,64]{1,0:T(8,128)} %copy-done.11) | copy-start | bytes 98308
  307.3 1.7 copy-start
  310.5 2.2 copy-start.3
  314.9 1.9 copy-start.4
  316.9 53.1 %collective-permute-start.1 = (bf16[128,1024]{0,1:T(8,128)(2,1)S(1)}, bf16[128,1024]{0,1:T(8,128)(2,1)S(1)}, u32[]{:S(2)}, u32[]{:S(2)}) collective-permute-start(bf16[128,1024]{0,1:T(8,128)(2,1)S(1)} %convert_element_type.143), channel_id=1, source_target_pairs={{0,1},{1,2},{2,3},{3,4},{4,5},{5,6},{6,7},{7,0},{8,9},{9,10},{10,1... | collective-permute-start | bytes 786440 | tf_op jit(solution)/shard_map/while/body/eval_jaxpr/ppermute | solution.py:19
  370.2 13.9 %collective-permute-start.1 = (bf16[128,1024]{0,1:T(8,128)(2,1)S(1)}, bf16[128,1024]{0,1:T(8,128)(2,1)S(1)}, u32[]{:S(2)}, u32[]{:S(2)}) collective-permute-start(bf16[128,1024]{0,1:T(8,128)(2,1)S(1)} %convert_element_type.143), channel_id=1, source_target_pairs={{0,1},{1,2},{2,3},{3,4},{4,5},{5,6},{6,7},{7,0},{8,9},{9,10},{10,1... | collective-permute-start | bytes 786440 | tf_op jit(solution)/shard_map/while/body/eval_jaxpr/ppermute | solution.py:19
  384.3 13.9 %collective-permute-start.1 = (bf16[128,1024]{0,1:T(8,128)(2,1)S(1)}, bf16[128,1024]{0,1:T(8,128)(2,1)S(1)}, u32[]{:S(2)}, u32[]{:S(2)}) collective-permute-start(bf16[128,1024]{0,1:T(8,128)(2,1)S(1)} %convert_element_type.143), channel_id=1, source_target_pairs={{0,1},{1,2},{2,3},{3,4},{4,5},{5,6},{6,7},{7,0},{8,9},{9,10},{10,1... | collective-permute-start | bytes 786440 | tf_op jit(solution)/shard_map/while/body/eval_jaxpr/ppermute | solution.py:19
  398.4 13.9 %collective-permute-start.1 = (bf16[128,1024]{0,1:T(8,128)(2,1)S(1)}, bf16[128,1024]{0,1:T(8,128)(2,1)S(1)}, u32[]{:S(2)}, u32[]{:S(2)}) collective-permute-start(bf16[128,1024]{0,1:T(8,128)(2,1)S(1)} %convert_element_type.143), channel_id=1, source_target_pairs={{0,1},{1,2},{2,3},{3,4},{4,5},{5,6},{6,7},{7,0},{8,9},{9,10},{10,1... | collective-permute-start | bytes 786440 | tf_op jit(solution)/shard_map/while/body/eval_jaxpr/ppermute | solution.py:19
  412.5 14.9 %collective-permute-start.1 = (bf16[128,1024]{0,1:T(8,128)(2,1)S(1)}, bf16[128,1024]{0,1:T(8,128)(2,1)S(1)}, u32[]{:S(2)}, u32[]{:S(2)}) collective-permute-start(bf16[128,1024]{0,1:T(8,128)(2,1)S(1)} %convert_element_type.143), channel_id=1, source_target_pairs={{0,1},{1,2},{2,3},{3,4},{4,5},{5,6},{6,7},{7,0},{8,9},{9,10},{10,1... | collective-permute-start | bytes 786440 | tf_op jit(solution)/shard_map/while/body/eval_jaxpr/ppermute | solution.py:19
  427.6 16.4 %collective-permute-start.1 = (bf16[128,1024]{0,1:T(8,128)(2,1)S(1)}, bf16[128,1024]{0,1:T(8,128)(2,1)S(1)}, u32[]{:S(2)}, u32[]{:S(2)}) collective-permute-start(bf16[128,1024]{0,1:T(8,128)(2,1)S(1)} %convert_element_type.143), channel_id=1, source_target_pairs={{0,1},{1,2},{2,3},{3,4},{4,5},{5,6},{6,7},{7,0},{8,9},{9,10},{10,1... | collective-permute-start | bytes 786440 | tf_op jit(solution)/shard_map/while/body/eval_jaxpr/ppermute | solution.py:19
  444.1 16.4 %collective-permute-start.1 = (bf16[128,1024]{0,1:T(8,128)(2,1)S(1)}, bf16[128,1024]{0,1:T(8,128)(2,1)S(1)}, u32[]{:S(2)}, u32[]{:S(2)}) collective-permute-start(bf16[128,1024]{0,1:T(8,128)(2,1)S(1)} %convert_element_type.143), channel_id=1, source_target_pairs={{0,1},{1,2},{2,3},{3,4},{4,5},{5,6},{6,7},{7,0},{8,9},{9,10},{10,1... | collective-permute-start | bytes 786440 | tf_op jit(solution)/shard_map/while/body/eval_jaxpr/ppermute | solution.py:19
  460.7 16.4 %collective-permute-start.1 = (bf16[128,1024]{0,1:T(8,128)(2,1)S(1)}, bf16[128,1024]{0,1:T(8,128)(2,1)S(1)}, u32[]{:S(2)}, u32[]{:S(2)}) collective-permute-start(bf16[128,1024]{0,1:T(8,128)(2,1)S(1)} %convert_element_type.143), channel_id=1, source_target_pairs={{0,1},{1,2},{2,3},{3,4},{4,5},{5,6},{6,7},{7,0},{8,9},{9,10},{10,1... | collective-permute-start | bytes 786440 | tf_op jit(solution)/shard_map/while/body/eval_jaxpr/ppermute | solution.py:19
  477.1 1.2 copy-start.6
  483.9 117.5 %reduce-scatter.7.cloned.1.call-start = ((), (), s32[]{:S(2)}) async-start(), calls=%async_computation.4 | async-start | bytes 1310720
Sparse Core Ops, SparseCore 0:
  484.1 87.7 reduce-scatter.4
  574.8 26.4 reduce-scatter.6
